TPU v7x, 256 devices: a whole 4x4x8 slice. The times are simulated.
256 devices in a mesh: pb: 16 (over z, core), kv: 16 (over y, x).
Axes of the slice: x: 4, y: 4, z: 8, core: 2. Of those that a mesh axis runs over, the one named last changes fastest.
Arguments:
- queries: bfloat16 [393216, 1024], P(('pb', 'kv')), may hold values from -8 to 8
- keys: bfloat16 [524288, 128], P(('kv', 'pb')), may hold values from -6 to 6
- values: bfloat16 [524288, 128], P(('kv', 'pb')), may hold values from -6 to 6
- selected: int32 [6144, 14], P(('pb', 'kv')), may hold values from 1 to 8190, as said below
Outputs:
- attended: bfloat16 [393216, 1024], P(('pb', 'kv'))
Inputs may be any that keep to these rules, and one draw needn't show every extreme that they name: `selected`: each row names 14 different blocks, never block 0 or block 8191. Key device k holds blocks k * 32 to (k + 1) * 32 - 1, devices counted with kv slowest; query device d holds query blocks d * 24 to (d + 1) * 24 - 1, devices counted with pb slowest. The query blocks of one device name together at most 2 distinct blocks of one key device, and in every draw some key device has exactly 2 named by every query device.
All inputs are finite; a program needn't handle non-finite values.
Results may differ from a plain program's by a relative error of at most 0.0046.
Values may be sent and summed in bfloat16 or wider, within the bound.
A program may use at most 128 MiB of HBM per device.

v0:
```python
import math
import jax
import jax.numpy as jnp
from jax import lax
from jax.sharding import PartitionSpec as P

H = 8
DH = 128
BLOCK = 64
TOPN = 16
QB = 64
CAP = 2


def holdings(wanted, owner, blocks_here):
    local_ids = owner * blocks_here + jnp.arange(blocks_here, dtype=jnp.int32)
    hits = (wanted[:, None] == local_ids[None, :]).astype(jnp.int32)
    present = jnp.max(hits, axis=0)
    return (present, jnp.cumsum(present) - present)


def slot_lists(present, slot_rank, slots):
    local_ids = jnp.arange(present.shape[-1], dtype=jnp.int32)
    slot_ids = jnp.arange(slots, dtype=jnp.int32)
    matches = (present[..., :, None] == 1) & (slot_rank[..., :, None] == slot_ids)
    return jnp.sum(jnp.where(matches, local_ids[:, None], 0), axis=-2)


def per_device(queries, keys, values, selected):
    pb_count = lax.axis_size("pb")
    kv_count = lax.axis_size("kv")
    devices = pb_count * kv_count
    blocks_here = keys.shape[0] // BLOCK
    query_blocks = queries.shape[0] // QB
    column_blocks = pb_count * blocks_here
    tiles_local = jnp.concatenate(
        [keys.reshape(blocks_here, BLOCK, DH), values.reshape(blocks_here, BLOCK, DH)], axis=2
    )
    column = lax.all_gather(tiles_local, "pb", axis=0, tiled=True)
    slots = CAP
    wanted = selected.reshape(-1)
    owners = jnp.arange(devices, dtype=jnp.int32)
    present, slot_rank = jax.vmap(lambda owner: holdings(wanted, owner, blocks_here))(owners)
    owner_lists = slot_lists(present, slot_rank, slots)
    by_column = (
        owner_lists.reshape(kv_count, pb_count, slots)
        + jnp.arange(pb_count, dtype=jnp.int32)[None, :, None] * blocks_here
    )
    by_column = by_column.reshape(kv_count, pb_count * slots)
    asked_for = lax.all_to_all(by_column, "kv", split_axis=0, concat_axis=0, tiled=True)
    me_kv = lax.axis_index("kv")
    end_pick = jnp.where(me_kv == kv_count - 1, column_blocks - 1, 0).astype(jnp.int32)
    picks = jnp.concatenate(
        [asked_for.reshape(kv_count, pb_count * slots), jnp.broadcast_to(end_pick, (kv_count, 1))],
        axis=1,
    )
    outgoing = jnp.take(column, picks.reshape(-1), axis=0).reshape(
        kv_count, pb_count * slots + 1, BLOCK, 2 * DH
    )
    fetched = lax.all_to_all(outgoing, "kv", split_axis=0, concat_axis=0, tiled=True)
    tile_table = fetched.reshape(devices * slots + kv_count, BLOCK, 2 * DH)
    owner_of = selected // blocks_here
    positions = owner_of * slots + jnp.take(slot_rank.reshape(-1), selected)
    positions = positions + owner_of // pb_count
    row = pb_count * slots + 1
    leading_positions = jnp.broadcast_to(
        jnp.array([row - 1, kv_count * row - 1], jnp.int32), (query_blocks, 2)
    )
    positions = jnp.concatenate([leading_positions, positions], axis=1)
    group_size = math.gcd(query_blocks, 8)
    q_groups = queries.reshape(query_blocks // group_size, group_size, QB * H, DH)
    p_groups = positions.reshape(query_blocks // group_size, group_size, TOPN)

    def attend(operands):
        q_block, positions_in = operands
        gathered = jnp.take(tile_table, positions_in.reshape(-1), axis=0).reshape(
            group_size, TOPN * BLOCK, 2 * DH
        )
        scores = jnp.einsum(
            "gqd,gkd->gqk", q_block, gathered[..., :DH], preferred_element_type=jnp.float32
        ) * DH ** (-0.5)
        weights = jnp.exp(scores - jnp.max(scores, axis=-1, keepdims=True))
        totals = jnp.sum(weights, axis=-1, keepdims=True)
        weighted = jnp.einsum(
            "gqk,gkd->gqd",
            weights.astype(jnp.bfloat16),
            gathered[..., DH:],
            preferred_element_type=jnp.float32,
        )
        return (weighted / totals).astype(jnp.bfloat16)

    result = lax.map(attend, (q_groups, p_groups))
    return result.reshape(query_blocks * QB, H * DH)


def solution(mesh):
    placed = (
        P(("pb", "kv"), None),
        P(("kv", "pb"), None),
        P(("kv", "pb"), None),
        P(("pb", "kv"), None),
    )
    return jax.shard_map(
        per_device, mesh=mesh, in_specs=placed, out_specs=P(("pb", "kv"), None), check_vma=False
    )
```

profile of v0, /device:TPU:1, one launch (start us, length us, event | category | flops | bytes accessed | tf_op | source)
XLA Modules:
  0.0 494.0 jit_solution(9905077446433948110)
XLA Ops:
  6.5 0.0 all-gather.2.cloned.1.call-start
  6.5 2.3 pad_maximum_fusion
  8.9 0.0 all-gather.2.cloned.1.call-update
  8.9 0.8 copy.30
  9.7 0.1 eq.42
  9.8 1.7 convert_reduce_fusion
  11.5 0.1 reduce_window_sum.11
  11.6 0.1 copy.38
  11.8 0.1 reshape.199
  11.9 0.1 add.109
  12.0 0.1 add.110
  12.1 0.6 broadcast_add_fusion
  12.7 7.6 %all-to-all-start = ((s32[16,1,32]{2,1,0:T(1,128)}), s32[16,1,32]{2,1,0:T(1,128)S(1)}, u32[]{:S(2)}, u32[]{:S(2)}) async-start(s32[16,1,32]{2,1,0:T(1,128)} %bitcast.6), calls=%async_computation | async-start | bytes 16384 | tf_op jit(solution)/shard_map/all_to_all | solution.py:50
  20.3 6.4 %all-to-all-done = s32[16,1,32]{2,1,0:T(1,128)S(1)} async-done(((s32[16,1,32]{2,1,0:T(1,128)}), s32[16,1,32]{2,1,0:T(1,128)S(1)}, u32[]{:S(2)}, u32[]{:S(2)}) %all-to-all-start) | async-done | bytes 2080 | tf_op jit(solution)/shard_map/all_to_all | solution.py:50
  26.7 0.1 reshape.202
  26.8 82.0 %all-gather.2.cloned.1.call-done = bf16[512,64,256]{2,1,0:T(8,128)(2,1)} async-done(((bf16[32,64,256]{2,1,0:T(8,128)(2,1)}), bf16[512,64,256]{2,1,0:T(8,128)(2,1)}) %all-gather.2.cloned.1.call-update) | async-done | bytes 16777232 | tf_op jit(solution)/shard_map/all_gather | solution.py:39
  108.9 21.2 %gather_fusion.2 = bf16[528,64,256]{2,1,0:T(8,128)(2,1)} fusion(bf16[512,64,256]{2,1,0:T(8,128)(2,1)} %all-gather.2.cloned.1.call-done, s32[1024]{0:T(1024)S(1)} %pad_clamp_fusion.1), kind=kCustom, calls=%fused_computation.2 | custom fusion | bytes 34605120 | tf_op jit(solution)/shard_map/jit(_take)/gather | solution.py:57
  130.1 14.4 %broadcast_select_fusion = bf16[16,33,64,256]{3,2,1,0:T(8,128)(2,1)} fusion(bf16[16,33,64,256]{3,2,1,0:T(8,128)(2,1)} %bitcast.37, pred[16,33]{1,0:T(8,128)(4,1)S(1)} %compare_and_fusion.1), kind=kLoop, calls=%fused_computation.26 | loop fusion | flops 8650752 | bytes 34603536 | tf_op jit(solution)/shard_map/jit(_take)/select_n | solution.py:57
  144.5 6.6 %all-to-all-start.1 = ((bf16[16,33,64,256]{3,2,1,0:T(8,128)(2,1)}), bf16[16,33,64,256]{3,2,1,0:T(8,128)(2,1)}, u32[]{:S(2)}, u32[]{:S(2)}) async-start(bf16[16,33,64,256]{3,2,1,0:T(8,128)(2,1)} %broadcast_select_fusion), calls=%async_computation.1 | async-start | bytes 34603008 | tf_op jit(solution)/shard_map/all_to_all | solution.py:60
  151.1 0.1 copy.37
  151.2 0.1 sub.31
  151.3 0.1 reshape.215
  151.4 0.0 copy-start
  151.5 2.5 gather_fusion.1
  154.0 0.1 reshape.214
  154.1 0.0 copy-done
  154.1 4.1 reshape.197
  158.3 0.1 add_bitcast_fusion
  158.4 251.6 %all-to-all-done.1 = bf16[16,33,64,256]{3,2,1,0:T(8,128)(2,1)} async-done(((bf16[16,33,64,256]{3,2,1,0:T(8,128)(2,1)}), bf16[16,33,64,256]{3,2,1,0:T(8,128)(2,1)}, u32[]{:S(2)}, u32[]{:S(2)}) %all-to-all-start.1) | async-done | bytes 17301536 | tf_op jit(solution)/shard_map/all_to_all | solution.py:60
  410.0 71.4 %while.10 = (s32[]{:T(128)}, bf16[3,8,512,128]{3,2,1,0:T(8,128)(2,1)}, bf16[3,8,512,128]{3,2,1,0:T(8,128)(2,1)S(1)}, s32[3,8,16]{2,1,0:T(8,128)S(1)}, bf16[528,64,256]{2,1,0:T(8,128)(2,1)}, /*index=5*/s32[]{:T(128)}) while((s32[]{:T(128)}, bf16[3,8,512,128]{3,2,1,0:T(8,128)(2,1)}, bf16[3,8,512,128]{3,2,1,0:T(8,128)(2,1)S(1)}, ...), condition=%wide.region_6.7_spmd, body=%wide.region_3.6_spmd.sunk | while | flops 2184177664 | bytes 73524040 | solution.py:92
  410.0 0.1 reshape.238
  410.1 8.7 %gather_fusion = bf16[128,64,256]{2,1,0:T(8,128)(2,1)} fusion(bf16[528,64,256]{2,1,0:T(8,128)(2,1)} %get-tuple-element.102, s32[1024]{0:T(1024)S(1)} %pad_clamp_fusion.4), kind=kCustom, calls=%fused_computation.clone.1 | custom fusion | bytes 8389120 | tf_op jit(solution)/shard_map/while/body/eval_jaxpr/jit(_take)/gather | solution.py:76
  418.8 0.1 broadcast_in_dim.86
  418.9 0.1 broadcast_in_dim.87
  419.0 4.6 bitcast_select_fusion.2
  423.6 2.4 multiply_reduce_fusion.2
  426.0 3.5 fusion.32
  429.5 4.3 bitcast_dynamic-update-slice_fusion.2
  433.8 0.1 reshape.238
  433.9 8.7 %gather_fusion = bf16[128,64,256]{2,1,0:T(8,128)(2,1)} fusion(bf16[528,64,256]{2,1,0:T(8,128)(2,1)} %get-tuple-element.102, s32[1024]{0:T(1024)S(1)} %pad_clamp_fusion.4), kind=kCustom, calls=%fused_computation.clone.1 | custom fusion | bytes 8389120 | tf_op jit(solution)/shard_map/while/body/eval_jaxpr/jit(_take)/gather | solution.py:76
  442.6 0.1 broadcast_in_dim.86
  442.7 0.1 broadcast_in_dim.87
  442.8 4.6 bitcast_select_fusion.2
  447.4 2.4 multiply_reduce_fusion.2
  449.8 3.5 fusion.32
  453.3 4.2 bitcast_dynamic-update-slice_fusion.2
  457.6 0.1 reshape.238
  457.7 8.7 %gather_fusion = bf16[128,64,256]{2,1,0:T(8,128)(2,1)} fusion(bf16[528,64,256]{2,1,0:T(8,128)(2,1)} %get-tuple-element.102, s32[1024]{0:T(1024)S(1)} %pad_clamp_fusion.4), kind=kCustom, calls=%fused_computation.clone.1 | custom fusion | bytes 8389120 | tf_op jit(solution)/shard_map/while/body/eval_jaxpr/jit(_take)/gather | solution.py:76
  466.4 0.1 broadcast_in_dim.86
  466.5 0.1 broadcast_in_dim.87
  466.6 4.6 bitcast_select_fusion.2
  471.1 2.4 multiply_reduce_fusion.2
  473.6 3.5 fusion.32
  477.1 4.2 bitcast_dynamic-update-slice_fusion.2
  481.4 5.8 %reshape.204 = bf16[1536,1024]{1,0:T(8,128)(2,1)} reshape(bf16[3,8,512,128]{3,2,1,0:T(8,128)(2,1)} %get-tuple-element.32) | data formatting | bytes 6291456 | tf_op jit(solution)/shard_map/reshape | solution.py:93
  (24 shorter events, 0.2 us)
Async XLA Ops:
  6.5 102.3 %all-gather.2.cloned.1.call-start = ((), (), s32[]{:S(2)}) async-start(), calls=%async_computation.2 | async-start | bytes 17825792 | tf_op jit(solution)/shard_map/all_gather | solution.py:39
  12.7 14.0 %all-to-all-start = ((s32[16,1,32]{2,1,0:T(1,128)}), s32[16,1,32]{2,1,0:T(1,128)S(1)}, u32[]{:S(2)}, u32[]{:S(2)}) async-start(s32[16,1,32]{2,1,0:T(1,128)} %bitcast.6), calls=%async_computation | async-start | bytes 16384 | tf_op jit(solution)/shard_map/all_to_all | solution.py:50
  144.5 265.4 %all-to-all-start.1 = ((bf16[16,33,64,256]{3,2,1,0:T(8,128)(2,1)}), bf16[16,33,64,256]{3,2,1,0:T(8,128)(2,1)}, u32[]{:S(2)}, u32[]{:S(2)}) async-start(bf16[16,33,64,256]{3,2,1,0:T(8,128)(2,1)} %broadcast_select_fusion), calls=%async_computation.1 | async-start | bytes 34603008 | tf_op jit(solution)/shard_map/all_to_all | solution.py:60
  151.4 2.7 copy-start
Sparse Core Ops, SparseCore 0:
  9.2 99.6 all-gather.1
where the time goes:
time: 495 us; the launch traced here: 494 us
  waiting for transfers between devices  340 us (69%)
  local copies, waits for them, and re-layouts  62.3 us (13%)
  other arithmetic  43.8 us (9%)
  matrix products  20 us (4%)
  starting transfers between devices  14.2 us (3%)
  between operations  13.6 us (3%)
    all_to_all x1, waiting for transfers between devices, per_device(): lax.all_to_all(outgoing, 'kv', split_axis=0, concat_axis=0, tiled=True)  252 us
    all_gather x1, waiting for transfers between devices, per_device(): column = lax.all_gather(tiles_local, 'pb', axis=0, tiled=True)  82 us
    gather x3, local copies, waits for them, and re-layouts, attend(): jnp.take(tile_table, positions_in.reshape(-1), axis=0)  26.1 us
    gather x1, local copies, waits for them, and re-layouts, per_device(): jnp.take(column, picks.reshape(-1), axis=0)  21.2 us
    select_n x2, other arithmetic, per_device(): jnp.take(column, picks.reshape(-1), axis=0)  14.5 us
    select_n x6, other arithmetic, attend(): jnp.take(tile_table, positions_in.reshape(-1), axis=0)  13.8 us
    dot_general x3, matrix products, attend(): jnp.einsum('gqk,gkd->gqd', weights.astype(jnp.bfloat16), gathered[..., DH...  12.7 us
    reduce_sum x3, other arithmetic, attend(): totals = jnp.sum(weights, axis=-1, keepdims=True)  10.6 us
  transfers between devices with their start and end apart: 3, of which 3 were waited for; matrix products, arithmetic and copies ran while one was open for 2% of the time, Pallas kernels for 0%

commit v1 on v0

--- a/solution.py
+++ b/solution.py
@@ -36,7 +36,9 @@
     tiles_local = jnp.concatenate(
         [keys.reshape(blocks_here, BLOCK, DH), values.reshape(blocks_here, BLOCK, DH)], axis=2
     )
-    column = lax.all_gather(tiles_local, "pb", axis=0, tiled=True)
+    column = jnp.concatenate(
+        lax.all_to_all(jnp.stack([tiles_local] * lax.axis_size("pb")), "pb", 0, 0), axis=0
+    )
     slots = CAP
     wanted = selected.reshape(-1)
     owners = jnp.arange(devices, dtype=jnp.int32)

time: 495 us -> 776 us (1.57)
  waiting for transfers between devices: 340 us -> 618 us
  between operations: 13.6 us -> 0.19 us
  starting transfers between devices: 14.2 us -> 23.3 us
    all_to_all x0 -> x1, waiting for transfers between devices: none -> 363 us  [per_device(): lax.all_to_all(jnp.stack([tiles_local] * lax.axis_size('pb')), 'pb', 0, 0)]
    all_gather x1 -> x0, waiting for transfers between devices: 82 us -> none  [per_device(): column = lax.all_gather(tiles_local, 'pb', axis=0, tiled=True)]
    all_to_all x0 -> x1, starting transfers between devices: none -> 10.6 us  [per_device(): lax.all_to_all(jnp.stack([tiles_local] * lax.axis_size('pb')), 'pb', 0, 0)]
  transfers between devices with their start and end apart: 3 -> 3, of which waited for: 3 -> 3; matrix products, arithmetic and copies ran while one was open for 2% -> 1% of each run, Pallas kernels for 0% -> 0%
where the time goes in v1:
time: 776 us; the launch traced here: 773 us
  waiting for transfers between devices  618 us (80%)
  local copies, waits for them, and re-layouts  68.2 us (9%)
  other arithmetic  42.8 us (6%)
  starting transfers between devices  23.3 us (3%)
  matrix products  20 us (3%)
    all_to_all x1, waiting for transfers between devices, per_device(): lax.all_to_all(jnp.stack([tiles_local] * lax.axis_size('pb')), 'pb', 0, 0)  363 us
    all_to_all x1, waiting for transfers between devices, per_device(): lax.all_to_all(outgoing, 'kv', split_axis=0, concat_axis=0, tiled=True)  250 us
    gather x3, local copies, waits for them, and re-layouts, attend(): jnp.take(tile_table, positions_in.reshape(-1), axis=0)  26.1 us
    gather x1, local copies, waits for them, and re-layouts, per_device(): jnp.take(column, picks.reshape(-1), axis=0)  21.2 us
  transfers between devices with their start and end apart: 3, of which 3 were waited for; matrix products, arithmetic and copies ran while one was open for 1% of the time, Pallas kernels for 0%

profile of v1, /device:TPU:1, one launch (start us, length us, event | category | flops | bytes accessed | tf_op | source)
XLA Modules:
  0.0 772.6 jit_solution(4852637744991415030)
XLA Ops:
  0.0 0.8 copy.30
  0.8 0.1 eq.42
  0.9 1.7 convert_reduce_fusion
  2.6 0.1 reduce_window_sum.11
  2.7 0.1 copy.38
  2.9 0.1 reshape.204
  3.0 0.1 add.109
  3.1 0.1 add.110
  3.2 0.6 broadcast_add_fusion
  3.8 7.6 all-to-all-start
  11.4 1.3 pad_maximum_fusion
  12.7 5.0 all-to-all-done
  17.7 5.9 stack.2
  23.6 10.6 %all-to-all-start.1 = ((bf16[16,32,64,256]{3,2,1,0:T(8,128)(2,1)}), bf16[16,32,64,256]{3,2,1,0:T(8,128)(2,1)}, u32[]{:S(2)}, u32[]{:S(2)}) async-start(bf16[16,32,64,256]{3,2,1,0:T(8,128)(2,1)} %stack.2), calls=%async_computation.1 | async-start | bytes 33554432 | tf_op jit(solution)/shard_map/all_to_all | solution.py:40
  34.2 0.1 reshape.208
  34.4 363.1 %all-to-all-done.1 = bf16[16,32,64,256]{3,2,1,0:T(8,128)(2,1)} async-done(((bf16[16,32,64,256]{3,2,1,0:T(8,128)(2,1)}), bf16[16,32,64,256]{3,2,1,0:T(8,128)(2,1)}, u32[]{:S(2)}, u32[]{:S(2)}) %all-to-all-start.1) | async-done | bytes 16777248 | tf_op jit(solution)/shard_map/all_to_all | solution.py:40
  397.5 21.2 %gather_fusion.2 = bf16[528,64,256]{2,1,0:T(8,128)(2,1)} fusion(bf16[512,64,256]{2,1,0:T(8,128)(2,1)} %bitcast.10, s32[1024]{0:T(1024)S(1)} %pad_clamp_fusion.1), kind=kCustom, calls=%fused_computation.2 | custom fusion | bytes 34605120 | tf_op jit(solution)/shard_map/jit(_take)/gather | solution.py:59
  418.7 14.4 %broadcast_select_fusion = bf16[16,33,64,256]{3,2,1,0:T(8,128)(2,1)} fusion(bf16[16,33,64,256]{3,2,1,0:T(8,128)(2,1)} %bitcast.38, pred[16,33]{1,0:T(8,128)(4,1)S(1)} %compare_and_fusion.1), kind=kLoop, calls=%fused_computation.26 | loop fusion | flops 8650752 | bytes 34603536 | tf_op jit(solution)/shard_map/jit(_take)/select_n | solution.py:59
  433.2 5.2 all-to-all-start.2
  438.3 0.0 copy-start
  438.3 0.1 copy.37
  438.4 0.1 sub.31
  438.6 0.1 reshape.221
  438.7 2.5 gather_fusion.1
  441.2 0.1 reshape.220
  441.3 0.0 copy-done
  441.3 4.1 reshape.202
  445.5 0.1 add_bitcast_fusion
  445.6 249.9 %all-to-all-done.2 = bf16[16,33,64,256]{3,2,1,0:T(8,128)(2,1)} async-done(((bf16[16,33,64,256]{3,2,1,0:T(8,128)(2,1)}), bf16[16,33,64,256]{3,2,1,0:T(8,128)(2,1)}, u32[]{:S(2)}, u32[]{:S(2)}) %all-to-all-start.2) | async-done | bytes 17301536 | tf_op jit(solution)/shard_map/all_to_all | solution.py:62
  695.5 71.4 %while.10 = (s32[]{:T(128)}, bf16[3,8,512,128]{3,2,1,0:T(8,128)(2,1)}, bf16[3,8,512,128]{3,2,1,0:T(8,128)(2,1)S(1)}, s32[3,8,16]{2,1,0:T(8,128)S(1)}, bf16[528,64,256]{2,1,0:T(8,128)(2,1)}, /*index=5*/s32[]{:T(128)}) while((s32[]{:T(128)}, bf16[3,8,512,128]{3,2,1,0:T(8,128)(2,1)}, bf16[3,8,512,128]{3,2,1,0:T(8,128)(2,1)S(1)}, ...), condition=%wide.region_6.7_spmd, body=%wide.region_3.6_spmd.sunk | while | flops 2184177664 | bytes 73524040 | solution.py:94
  695.5 0.1 reshape.244
  695.6 8.7 %gather_fusion = bf16[128,64,256]{2,1,0:T(8,128)(2,1)} fusion(bf16[528,64,256]{2,1,0:T(8,128)(2,1)} %get-tuple-element.102, s32[1024]{0:T(1024)S(1)} %pad_clamp_fusion.4), kind=kCustom, calls=%fused_computation.clone.1 | custom fusion | bytes 8389120 | tf_op jit(solution)/shard_map/while/body/eval_jaxpr/jit(_take)/gather | solution.py:78
  704.3 0.1 broadcast_in_dim.86
  704.4 0.1 broadcast_in_dim.87
  704.5 4.6 bitcast_select_fusion.2
  709.1 2.4 multiply_reduce_fusion.2
  711.5 3.5 fusion.32
  715.0 4.3 bitcast_dynamic-update-slice_fusion.2
  719.3 0.1 reshape.244
  719.4 8.7 %gather_fusion = bf16[128,64,256]{2,1,0:T(8,128)(2,1)} fusion(bf16[528,64,256]{2,1,0:T(8,128)(2,1)} %get-tuple-element.102, s32[1024]{0:T(1024)S(1)} %pad_clamp_fusion.4), kind=kCustom, calls=%fused_computation.clone.1 | custom fusion | bytes 8389120 | tf_op jit(solution)/shard_map/while/body/eval_jaxpr/jit(_take)/gather | solution.py:78
  728.1 0.1 broadcast_in_dim.86
  728.2 0.1 broadcast_in_dim.87
  728.3 4.6 bitcast_select_fusion.2
  732.9 2.4 multiply_reduce_fusion.2
  735.3 3.5 fusion.32
  738.8 4.2 bitcast_dynamic-update-slice_fusion.2
  743.1 0.1 reshape.244
  743.2 8.7 %gather_fusion = bf16[128,64,256]{2,1,0:T(8,128)(2,1)} fusion(bf16[528,64,256]{2,1,0:T(8,128)(2,1)} %get-tuple-element.102, s32[1024]{0:T(1024)S(1)} %pad_clamp_fusion.4), kind=kCustom, calls=%fused_computation.clone.1 | custom fusion | bytes 8389120 | tf_op jit(solution)/shard_map/while/body/eval_jaxpr/jit(_take)/gather | solution.py:78
  751.9 0.1 broadcast_in_dim.86
  752.0 0.1 broadcast_in_dim.87
  752.1 4.6 bitcast_select_fusion.2
  756.6 2.4 multiply_reduce_fusion.2
  759.1 3.5 fusion.32
  762.6 4.2 bitcast_dynamic-update-slice_fusion.2
  766.9 5.8 reshape.210
  (24 shorter events, 0.2 us)
Async XLA Ops:
  3.8 13.9 %all-to-all-start = ((s32[16,1,32]{2,1,0:T(1,128)}), s32[16,1,32]{2,1,0:T(1,128)S(1)}, u32[]{:S(2)}, u32[]{:S(2)}) async-start(s32[16,1,32]{2,1,0:T(1,128)} %bitcast.6), calls=%async_computation | async-start | bytes 16384 | tf_op jit(solution)/shard_map/all_to_all | solution.py:52
  23.6 373.8 %all-to-all-start.1 = ((bf16[16,32,64,256]{3,2,1,0:T(8,128)(2,1)}), bf16[16,32,64,256]{3,2,1,0:T(8,128)(2,1)}, u32[]{:S(2)}, u32[]{:S(2)}) async-start(bf16[16,32,64,256]{3,2,1,0:T(8,128)(2,1)} %stack.2), calls=%async_computation.1 | async-start | bytes 33554432 | tf_op jit(solution)/shard_map/all_to_all | solution.py:40
  433.2 262.3 %all-to-all-start.2 = ((bf16[16,33,64,256]{3,2,1,0:T(8,128)(2,1)}), bf16[16,33,64,256]{3,2,1,0:T(8,128)(2,1)}, u32[]{:S(2)}, u32[]{:S(2)}) async-start(bf16[16,33,64,256]{3,2,1,0:T(8,128)(2,1)} %broadcast_select_fusion), calls=%async_computation.2 | async-start | bytes 34603008 | tf_op jit(solution)/shard_map/all_to_all | solution.py:62
  438.3 3.0 copy-start
